TPU v7x, 1024 devices: a whole 8x8x8 slice. The times are simulated.
1024 devices in a mesh: expert: 64 (over y, z), section: 16 (over x, core).
Axes of the slice: x: 8, y: 8, z: 8, core: 2. Of those that a mesh axis runs over, the one named last changes fastest.
Arguments:
- section_acts: bfloat16 [16, 12288, 256], P('section', 'expert'), may hold values from -6 to 6
- section_input_gradients: bfloat16 [16, 12288, 256], P('section', 'expert'), may hold values from -6 to 6
- saved_input: bfloat16 [16, 12288, 256], P('section', 'expert'), may hold values from -6 to 6
- fwd_routes: int32 [16, 768, 8], P('section'), may hold values from 0 to 255, all different within a row; in each aligned block of 192 rows (0 to 191, 192 to 383, ..., all dimensions but the last counted through in order) at most 12 rows name the same one
- fwd_probs: float32 [16, 768, 8], P('section'), may hold values from 0.1 to 1
- back_routes: int32 [16, 768, 8], P('section'), may hold values from 0 to 255, all different within a row; in each aligned block of 192 rows (0 to 191, 192 to 383, ..., all dimensions but the last counted through in order) at most 12 rows name the same one
- back_probs: float32 [16, 768, 8], P('section'), may hold values from 0.1 to 1
- w_gate: bfloat16 [16, 8192, 4096], P('section', 'expert'), may hold values from -0.09375 to 0.09375
- w_up: bfloat16 [16, 8192, 4096], P('section', 'expert'), may hold values from -0.09375 to 0.09375
- w_down: bfloat16 [16, 8192, 4096], P('section', 'expert'), may hold values from -0.125 to 0.125
Outputs:
- section_out: bfloat16 [16, 12288, 256], P('section', 'expert')
- input_grads: bfloat16 [16, 12288, 256], P('section', 'expert')
Inputs may be any that keep to these rules, and one draw needn't show every extreme that they name: `fwd_routes`: in each aligned block of 192 rows (one group of one section) no id is named by more than 12 rows, and some block has an id named by exactly 12; every id is named somewhere. `back_routes`: in each aligned block of 192 rows (one group of one section) no id is named by more than 12 rows, and some block has an id named by exactly 12; every id is named somewhere.
All inputs are finite; a program needn't handle non-finite values.
Results may differ from a plain program's by a relative error of at most 0.0075.
Values may be sent and summed in bfloat16 or wider, within the bound.
A program may use at most 32 MiB of HBM per device.

v0:
```python
import jax
import jax.numpy as jnp
from jax import lax
from jax.sharding import PartitionSpec as P

N_ROUTED = 256
TOP = 8
E_WIN = 4


def from_behind(x, axis, by):
    peers = lax.axis_size(axis)
    return lax.ppermute(x, axis, [(i, (i + by) % peers) for i in range(peers)])


def route_tables(routes, probs, first, count):
    capacity = count * TOP * 2 // N_ROUTED
    block = lax.dynamic_slice_in_dim(routes, first, count, 0)
    gains = lax.dynamic_slice_in_dim(probs, first, count, 0)
    labels = jnp.arange(E_WIN, dtype=jnp.int32)
    hits = block[:, :, None] == labels[None, None, :]
    chosen = jnp.sum(hits.astype(jnp.int32), axis=1, dtype=jnp.int32)
    weight = jnp.sum(jnp.where(hits, gains[:, :, None], jnp.float32(0.0)), axis=1)
    before = jnp.cumsum(chosen, axis=0, dtype=jnp.int32) - chosen
    places = jnp.arange(capacity, dtype=jnp.int32)
    mask = (before[:, None, :] == places[None, :, None]) & (chosen[:, None, :] > 0)
    picker = mask.astype(jnp.float32).reshape(count, capacity * E_WIN)
    weighted = jnp.where(mask, weight[:, None, :], jnp.float32(0.0)).reshape(
        count, capacity * E_WIN
    )
    return (picker, weighted)


def pick_rows(picker, values):
    return jnp.einsum(
        "tm,td->md", picker.astype(jnp.bfloat16), values, preferred_element_type=jnp.float32
    )


def fan_out(rows, split):
    width = rows.shape[1]
    capacity = rows.shape[0] // E_WIN
    spread = jnp.broadcast_to(
        rows.reshape(capacity, E_WIN, 1, width), (capacity, E_WIN, split, width)
    )
    return spread.reshape(capacity, E_WIN * split, width)


def expert_rows(piece):
    count = piece.shape[0]
    return piece.reshape(count * E_WIN, piece.shape[1] * piece.shape[2] // E_WIN)


def slot_layout(rows, count, width):
    return rows.reshape(count, rows.shape[1] // width * E_WIN, width)


def fold_slices(received, split):
    count = received.shape[0]
    width = received.shape[2]
    summed = jnp.sum(received.reshape(count, E_WIN, split, width).astype(jnp.float32), axis=2)
    return summed.reshape(count * E_WIN, width)


def forward_rows(rows, gate_w, up_w, down_w):
    gate_pre = jnp.einsum("md,hd->mh", rows, gate_w, preferred_element_type=jnp.float32)
    up_pre = jnp.einsum("md,hd->mh", rows, up_w, preferred_element_type=jnp.float32)
    hidden = (jax.nn.silu(gate_pre) * up_pre).astype(jnp.bfloat16)
    return jnp.dot(hidden, down_w, preferred_element_type=jnp.float32).astype(jnp.bfloat16)


def backward_rows(rows, scaled, gate_w, up_w, down_w):
    gate_pre = jnp.einsum("md,hd->mh", rows, gate_w, preferred_element_type=jnp.float32)
    up_pre = jnp.einsum("md,hd->mh", rows, up_w, preferred_element_type=jnp.float32)
    sig = jax.nn.sigmoid(gate_pre)
    act = gate_pre * sig
    d_hidden = jnp.einsum("md,hd->mh", scaled, down_w, preferred_element_type=jnp.float32)
    d_up = (d_hidden * act).astype(jnp.bfloat16)
    d_gate = (d_hidden * up_pre * sig * (1.0 + gate_pre * (1.0 - sig))).astype(jnp.bfloat16)
    back = jnp.dot(d_gate, gate_w, preferred_element_type=jnp.float32) + jnp.dot(
        d_up, up_w, preferred_element_type=jnp.float32
    )
    return back.astype(jnp.bfloat16)


def shards(
    section_acts,
    section_input_gradients,
    saved_input,
    fwd_routes,
    fwd_probs,
    back_routes,
    back_probs,
    w_gate,
    w_up,
    w_down,
):
    split = lax.axis_size("expert") // E_WIN
    group = lax.axis_index("expert") // split
    x_in = from_behind(section_acts, "section", 1)[0]
    dy_in = from_behind(section_input_gradients, "section", -1)[0]
    backward_input = saved_input[0]
    count = x_in.shape[0]
    width = x_in.shape[1]
    gate_w = w_gate[0]
    up_w = w_up[0]
    down_w = w_down[0]
    f_pick, f_weight = route_tables(fwd_routes[0], fwd_probs[0], group * count, count)
    b_pick, b_weight = route_tables(back_routes[0], back_probs[0], group * count, count)
    scale = jnp.sum(b_weight, axis=0)
    fwd_send = fan_out(pick_rows(f_pick, x_in).astype(jnp.bfloat16), split)
    backward_outbound = fan_out(pick_rows(b_pick, backward_input).astype(jnp.bfloat16), split)
    grad_send = fan_out((pick_rows(b_pick, dy_in) * scale[:, None]).astype(jnp.bfloat16), split)
    piece = lax.all_to_all(fwd_send, "expert", split_axis=1, concat_axis=1, tiled=True)
    slots = piece.shape[0]
    made = forward_rows(expert_rows(piece), gate_w, up_w, down_w)
    made_back = lax.all_to_all(
        slot_layout(made, slots, width), "expert", split_axis=1, concat_axis=1, tiled=True
    )
    pieces = (
        lax.all_to_all(backward_outbound, "expert", split_axis=1, concat_axis=1, tiled=True),
        lax.all_to_all(grad_send, "expert", split_axis=1, concat_axis=1, tiled=True),
    )
    slots = pieces[0].shape[0]
    back = backward_rows(expert_rows(pieces[0]), expert_rows(pieces[1]), gate_w, up_w, down_w)
    grad_back = lax.all_to_all(
        slot_layout(back, slots, width), "expert", split_axis=1, concat_axis=1, tiled=True
    )
    high = lax.Precision.HIGHEST
    moe = jnp.dot(f_weight, fold_slices(made_back, split), precision=high)
    dx_moe = jnp.dot(b_pick, fold_slices(grad_back, split), precision=high)
    section_out = (x_in.astype(jnp.float32) + moe).astype(jnp.bfloat16)
    input_grads = (dy_in.astype(jnp.float32) + dx_moe).astype(jnp.bfloat16)
    return (section_out[None], input_grads[None])


def solution(mesh):
    return jax.shard_map(
        shards,
        mesh=mesh,
        in_specs=(
            P("section", "expert", None),
            P("section", "expert", None),
            P("section", "expert", None),
            P("section", None, None),
            P("section", None, None),
            P("section", None, None),
            P("section", None, None),
            P("section", "expert", None),
            P("section", "expert", None),
            P("section", "expert", None),
        ),
        out_specs=(P("section", "expert", None), P("section", "expert", None)),
        check_vma=False,
    )
```

profile of v0, /device:TPU:14, one launch (start us, length us, event | category | flops | bytes accessed | tf_op | source)
XLA Modules:
  0.0 148.9 jit_solution(8474284928927521989)
XLA Ops:
  0.6 0.0 copy-start
  0.6 0.9 collective-permute-start.1
  1.5 0.8 dynamic-slice_bitcast_fusion.1
  2.4 1.2 reduce-window.16
  3.6 0.1 slice.26
  3.7 0.1 copy.75
  3.8 0.1 copy.76
  3.9 0.1 add_bitcast_fusion
  4.0 0.6 fusion.32
  4.7 0.1 convolution_convert_fusion.1
  4.9 0.8 broadcast_in_dim.96
  5.7 23.5 %all-to-all-start.3 = ((bf16[12,64,256]{2,0,1:T(8,128)(2,1)}), bf16[12,64,256]{2,0,1:T(8,128)(2,1)S(1)}, u32[]{:S(2)}, u32[]{:S(2)}) async-start(bf16[12,64,256]{2,0,1:T(8,128)(2,1)} %bitcast.21), calls=%async_computation.3 | async-start | bytes 1048576 | tf_op jit(solution)/shard_map/all_to_all | solution.py:121
  29.2 0.0 collective-permute-start
  29.3 1.2 reduce-window.14
  30.5 0.1 slice.24
  30.6 0.1 copy.67
  30.8 0.1 copy.68
  30.9 0.1 add_bitcast_fusion.1
  30.9 1.4 dynamic-slice_bitcast_fusion
  32.4 0.1 select_reduce_fusion
  32.5 0.1 mul.42
  32.6 0.0 copy-start.6
  32.6 0.1 fusion.1
  32.7 0.1 broadcast_in_dim.93
  32.7 0.5 copy-done.6
  33.2 15.0 %all-to-all-done.3 = bf16[12,64,256]{2,0,1:T(8,128)(2,1)S(1)} async-done(((bf16[12,64,256]{2,0,1:T(8,128)(2,1)}), bf16[12,64,256]{2,0,1:T(8,128)(2,1)S(1)}, u32[]{:S(2)}, u32[]{:S(2)}) %all-to-all-start.3) | async-done | bytes 393248 | tf_op jit(solution)/shard_map/all_to_all | solution.py:121
  48.2 0.8 broadcast_in_dim.94
  49.1 5.4 %all-to-all-start.2 = ((bf16[12,64,256]{2,0,1:T(8,128)(2,1)}), bf16[12,64,256]{2,0,1:T(8,128)(2,1)S(1)}, u32[]{:S(2)}, u32[]{:S(2)}) async-start(bf16[12,64,256]{2,0,1:T(8,128)(2,1)} %bitcast.19), calls=%async_computation.2 | async-start | bytes 1048576 | tf_op jit(solution)/shard_map/all_to_all | solution.py:122
  54.5 0.0 copy-start.1
  54.6 0.0 copy-start.8
  54.6 0.1 convolution_convert_fusion.2
  54.7 0.5 copy-done.8
  55.2 0.6 copy.69
  55.8 0.9 copy.80
  56.7 1.2 reshape.208
  57.9 1.1 fusion.16
  59.0 14.3 %all-to-all-done.2 = bf16[12,64,256]{2,0,1:T(8,128)(2,1)S(1)} async-done(((bf16[12,64,256]{2,0,1:T(8,128)(2,1)}), bf16[12,64,256]{2,0,1:T(8,128)(2,1)S(1)}, u32[]{:S(2)}, u32[]{:S(2)}) %all-to-all-start.2) | async-done | bytes 393248 | tf_op jit(solution)/shard_map/all_to_all | solution.py:122
  73.2 0.9 broadcast_in_dim.88
  74.1 0.1 copy-done.3
  74.2 5.6 %all-to-all-start = ((bf16[12,64,256]{2,0,1:T(8,128)(2,1)}), bf16[12,64,256]{2,0,1:T(8,128)(2,1)}, u32[]{:S(2)}, u32[]{:S(2)}) async-start(bf16[12,64,256]{2,0,1:T(8,128)(2,1)} %bitcast.6), calls=%async_computation | async-start | bytes 1048576 | tf_op jit(solution)/shard_map/all_to_all | solution.py:114
  79.9 0.0 copy-start.2
  79.9 2.0 %copy.78 = bf16[12,64,256]{2,1,0:T(8,128)(2,1)} copy(bf16[12,64,256]{2,0,1:T(8,128)(2,1)} %copy-done.3) | data formatting | bytes 786432 | tf_op jit(solution)/shard_map/all_to_all | solution.py:122
  81.9 1.9 %reshape.206 = bf16[48,4096]{1,0:T(8,128)(2,1)} reshape(bf16[12,64,256]{2,1,0:T(8,128)(2,1)} %copy.78) | data formatting | bytes 786432 | tf_op jit(solution)/shard_map/reshape | solution.py:51
  83.8 2.1 %fusion.7 = f32[48,128]{1,0:T(8,128)} fusion(bf16[48,4096]{1,0:T(8,128)(2,1)} %reshape.206, bf16[1,128,4096]{2,1,0:T(8,128)(2,1)S(1)} %copy-done.2), kind=kOutput, calls=%fused_computation.18 | convolution fusion | flops 50331648 | bytes 1466368 | tf_op jit(solution)/shard_map/md,hd->mh/dot_general | solution.py:77
  85.9 2.6 %fusion.6 = f32[48,4096]{1,0:T(8,128)} fusion(f32[48,128]{1,0:T(8,128)} %fusion.7, bf16[48,4096]{1,0:T(8,128)(2,1)S(1)} %reshape.208, bf16[1,128,4096]{2,1,0:T(8,128)(2,1)S(1)} %copy-done, bf16[1,128,4096]{2,1,0:T(8,128)(2,1)S(1)} %copy-done.1, f32[48,128]{1,0:T(8,128)} %fusion.16), kind=kOutput, calls=%fused_computation.15 | convolution fusion | flops 100724736 | bytes 3325952 | tf_op jit(solution)/shard_map/dot_general | solution.py:80
  88.5 2.2 %fusion = bf16[48,4096]{1,0:T(8,128)(2,1)} fusion(f32[48,4096]{1,0:T(8,128)} %fusion.6, bf16[1,128,4096]{2,1,0:T(8,128)(2,1)S(1)} %copy-done, f32[48,128]{1,0:T(8,128)} %fusion.7, f32[48,128]{1,0:T(8,128)} %fusion.16), kind=kOutput, calls=%fused_computation.1 | convolution fusion | flops 50761728 | bytes 2277376 | tf_op jit(solution)/shard_map/dot_general | solution.py:80
  90.7 1.2 reshape.209
  91.9 1.0 copy.81
  92.9 5.2 %all-to-all-done = bf16[12,64,256]{2,0,1:T(8,128)(2,1)} async-done(((bf16[12,64,256]{2,0,1:T(8,128)(2,1)}), bf16[12,64,256]{2,0,1:T(8,128)(2,1)}, u32[]{:S(2)}, u32[]{:S(2)}) %all-to-all-start) | async-done | bytes 393248 | tf_op jit(solution)/shard_map/all_to_all | solution.py:114
  98.1 7.7 %all-to-all-start.4 = ((bf16[12,64,256]{2,0,1:T(8,128)(2,1)}), bf16[12,64,256]{2,0,1:T(8,128)(2,1)}, u32[]{:S(2)}, u32[]{:S(2)}) async-start(bf16[12,64,256]{2,0,1:T(8,128)(2,1)} %copy.81), calls=%async_computation.4 | async-start | bytes 1048576 | tf_op jit(solution)/shard_map/all_to_all | solution.py:126
  105.8 1.9 %copy.70 = bf16[12,64,256]{2,1,0:T(8,128)(2,1)} copy(bf16[12,64,256]{2,0,1:T(8,128)(2,1)} %all-to-all-done) | data formatting | bytes 786432 | tf_op jit(solution)/shard_map/all_to_all | solution.py:114
  107.7 1.2 reshape.201
  108.9 1.1 fusion.18
  110.0 1.6 %convolution_convert_fusion = bf16[48,4096]{1,0:T(8,128)(2,1)S(1)} fusion(bf16[48,4096]{1,0:T(8,128)(2,1)S(1)} %reshape.201, bf16[1,128,4096]{2,1,0:T(8,128)(2,1)S(1)} %copy-done.2, bf16[1,128,4096]{2,1,0:T(8,128)(2,1)S(1)} %copy-done, f32[48,128]{1,0:T(8,128)} %fusion.18), kind=kOutput, calls=%fused_computation.2 | convolution fusion | flops 100896768 | bytes 2908160 | tf_op jit(solution)/shard_map/dot_general | solution.py:69
  111.6 0.2 reshape.202
  111.8 1.0 copy.71
  112.8 10.9 %all-to-all-done.4 = bf16[12,64,256]{2,0,1:T(8,128)(2,1)} async-done(((bf16[12,64,256]{2,0,1:T(8,128)(2,1)}), bf16[12,64,256]{2,0,1:T(8,128)(2,1)}, u32[]{:S(2)}, u32[]{:S(2)}) %all-to-all-start.4) | async-done | bytes 393248 | tf_op jit(solution)/shard_map/all_to_all | solution.py:126
  123.7 5.1 %all-to-all-start.1 = ((bf16[12,64,256]{2,0,1:T(8,128)(2,1)}), bf16[12,64,256]{2,0,1:T(8,128)(2,1)S(1)}, u32[]{:S(2)}, u32[]{:S(2)}) async-start(bf16[12,64,256]{2,0,1:T(8,128)(2,1)} %copy.71), calls=%async_computation.1 | async-start | bytes 1048576 | tf_op jit(solution)/shard_map/all_to_all | solution.py:117
  128.9 1.1 convert_reduce_fusion
  130.0 0.0 copy-start.7
  130.1 16.8 %all-to-all-done.1 = bf16[12,64,256]{2,0,1:T(8,128)(2,1)S(1)} async-done(((bf16[12,64,256]{2,0,1:T(8,128)(2,1)}), bf16[12,64,256]{2,0,1:T(8,128)(2,1)S(1)}, u32[]{:S(2)}, u32[]{:S(2)}) %all-to-all-start.1) | async-done | bytes 393248 | tf_op jit(solution)/shard_map/all_to_all | solution.py:117
  146.8 0.1 convert_reduce_fusion.1
  147.0 0.9 fusion.21
  147.9 1.0 fusion.20
  (45 shorter events, 0.4 us)
Async XLA Ops:
  0.6 85.3 %copy-start = (bf16[1,128,4096]{2,1,0:T(8,128)(2,1)S(1)}, bf16[1,128,4096]{2,1,0:T(8,128)(2,1)}, u32[]{:S(2)}) copy-start(bf16[1,128,4096]{2,1,0:T(8,128)(2,1)} %param.18) | copy-start | bytes 3145732
  0.6 31.9 %collective-permute-start.1 = (bf16[1,192,256]{2,1,0:T(8,128)(2,1)}, bf16[1,192,256]{2,1,0:T(8,128)(2,1)S(1)}, u32[]{:S(2)}, u32[]{:S(2)}) collective-permute-start(bf16[1,192,256]{2,1,0:T(8,128)(2,1)} %param.11), channel_id=1, source_target_pairs={{0,15},{1,0},{2,1},{3,2},{4,3},{5,4},{6,5},{7,6},{8,7},{9,8},{10,9... | collective-permute-start | bytes 294920 | tf_op jit(solution)/shard_map/ppermute | solution.py:13
  2.3 2.4 %copy-start.5 = (bf16[1,192,256]{2,1,0:T(8,128)(2,1)S(1)}, bf16[1,192,256]{2,1,0:T(8,128)(2,1)}, u32[]{:S(2)}) copy-start(bf16[1,192,256]{2,1,0:T(8,128)(2,1)} %param.12) | copy-start | bytes 294916
  5.7 23.6 %copy-start.12 = (bf16[1,192,256]{2,1,0:T(8,128)(2,1)S(1)}, bf16[1,192,256]{2,1,0:T(8,128)(2,1)}, u32[]{:S(2)}) copy-start(bf16[1,192,256]{2,1,0:T(8,128)(2,1)} %param.10) | copy-start | bytes 294916
  5.7 42.6 %all-to-all-start.3 = ((bf16[12,64,256]{2,0,1:T(8,128)(2,1)}), bf16[12,64,256]{2,0,1:T(8,128)(2,1)S(1)}, u32[]{:S(2)}, u32[]{:S(2)}) async-start(bf16[12,64,256]{2,0,1:T(8,128)(2,1)} %bitcast.21), calls=%async_computation.3 | async-start | bytes 1048576 | tf_op jit(solution)/shard_map/all_to_all | solution.py:121
  29.2 25.3 %collective-permute-start = (bf16[1,192,256]{2,1,0:T(8,128)(2,1)S(1)}, bf16[1,192,256]{2,1,0:T(8,128)(2,1)S(1)}, u32[]{:S(2)}, u32[]{:S(2)}) collective-permute-start(bf16[1,192,256]{2,1,0:T(8,128)(2,1)S(1)} %copy-done.12), channel_id=1, source_target_pairs={{0,1},{1,2},{2,3},{3,4},{4,5},{5,6},{6,7},{7,8},{8,9},{9,10},{10,1... | collective-permute-start | bytes 294920 | tf_op jit(solution)/shard_map/ppermute | solution.py:13
  32.6 0.6 copy-start.6
  49.1 24.2 %all-to-all-start.2 = ((bf16[12,64,256]{2,0,1:T(8,128)(2,1)}), bf16[12,64,256]{2,0,1:T(8,128)(2,1)S(1)}, u32[]{:S(2)}, u32[]{:S(2)}) async-start(bf16[12,64,256]{2,0,1:T(8,128)(2,1)} %bitcast.19), calls=%async_computation.2 | async-start | bytes 1048576 | tf_op jit(solution)/shard_map/all_to_all | solution.py:122
  54.5 3.4 %copy-start.1 = (bf16[1,128,4096]{2,1,0:T(8,128)(2,1)S(1)}, bf16[1,128,4096]{2,1,0:T(8,128)(2,1)}, u32[]{:S(2)}) copy-start(bf16[1,128,4096]{2,1,0:T(8,128)(2,1)} %param.17) | copy-start | bytes 3145732
  54.6 0.6 copy-start.8
  57.9 15.4 %copy-start.4 = (bf16[12,4,256]{2,0,1:T(8,128)(2,1)S(1)}, bf16[12,4,256]{2,0,1:T(8,128)(2,1)}, u32[]{:S(2)}) copy-start(bf16[12,4,256]{2,0,1:T(8,128)(2,1)} %copy.69) | copy-start | bytes 73732
  73.2 1.0 copy-start.3
  74.2 23.9 %all-to-all-start = ((bf16[12,64,256]{2,0,1:T(8,128)(2,1)}), bf16[12,64,256]{2,0,1:T(8,128)(2,1)}, u32[]{:S(2)}, u32[]{:S(2)}) async-start(bf16[12,64,256]{2,0,1:T(8,128)(2,1)} %bitcast.6), calls=%async_computation | async-start | bytes 1048576 | tf_op jit(solution)/shard_map/all_to_all | solution.py:114
  79.9 4.0 %copy-start.2 = (bf16[1,128,4096]{2,1,0:T(8,128)(2,1)S(1)}, bf16[1,128,4096]{2,1,0:T(8,128)(2,1)}, u32[]{:S(2)}) copy-start(bf16[1,128,4096]{2,1,0:T(8,128)(2,1)} %param.19) | copy-start | bytes 3145732
  98.1 25.6 %all-to-all-start.4 = ((bf16[12,64,256]{2,0,1:T(8,128)(2,1)}), bf16[12,64,256]{2,0,1:T(8,128)(2,1)}, u32[]{:S(2)}, u32[]{:S(2)}) async-start(bf16[12,64,256]{2,0,1:T(8,128)(2,1)} %copy.81), calls=%async_computation.4 | async-start | bytes 1048576 | tf_op jit(solution)/shard_map/all_to_all | solution.py:126
  112.8 16.0 %copy-start.10 = (f32[192,8]{0,1:T(8,128)S(1)}, f32[192,8]{0,1:T(8,128)}, u32[]{:S(2)}) copy-start(f32[192,8]{0,1:T(8,128)} %get-tuple-element.5) | copy-start | bytes 18436
  123.7 23.1 %all-to-all-start.1 = ((bf16[12,64,256]{2,0,1:T(8,128)(2,1)}), bf16[12,64,256]{2,0,1:T(8,128)(2,1)S(1)}, u32[]{:S(2)}, u32[]{:S(2)}) async-start(bf16[12,64,256]{2,0,1:T(8,128)(2,1)} %copy.71), calls=%async_computation.1 | async-start | bytes 1048576 | tf_op jit(solution)/shard_map/all_to_all | solution.py:117
  130.0 16.9 %copy-start.7 = (bf16[1,192,256]{2,1,0:T(8,128)(2,1)S(1)}, bf16[1,192,256]{2,1,0:T(8,128)(2,1)}, u32[]{:S(2)}) copy-start(bf16[1,192,256]{2,1,0:T(8,128)(2,1)} %copy-done.6) | copy-start | bytes 294916
  130.1 16.9 %copy-start.11 = (pred[192,12,4]{0,2,1:T(4,128)(4,1)S(1)}, pred[192,12,4]{0,2,1:T(4,128)(4,1)}, u32[]{:S(2)}) copy-start(pred[192,12,4]{0,2,1:T(4,128)(4,1)} %get-tuple-element.2) | copy-start | bytes 27652
  147.0 1.0 copy-start.9
where the time goes:
time: 151 us; the launch traced here: 149 us
  waiting for transfers between devices  62.1 us (41%)
  starting transfers between devices  48.3 us (32%)
  local copies, waits for them, and re-layouts  19.7 us (13%)
  matrix products  13 us (9%)
  other arithmetic  4.78 us (3%)
    all_to_all x1, starting transfers between devices, shards(): lax.all_to_all(backward_outbound, 'expert', split_axis=1, concat_axis=1,...  23.5 us
    all_to_all x1, waiting for transfers between devices, shards(): lax.all_to_all(slot_layout(made, slots, width), 'expert', split_axis=1, c...  16.8 us
    all_to_all x1, waiting for transfers between devices, shards(): lax.all_to_all(backward_outbound, 'expert', split_axis=1, concat_axis=1,...  15 us
    all_to_all x1, waiting for transfers between devices, shards(): lax.all_to_all(grad_send, 'expert', split_axis=1, concat_axis=1, tiled=True)  14.3 us
    all_to_all x1, waiting for transfers between devices, shards(): lax.all_to_all(slot_layout(back, slots, width), 'expert', split_axis=1, c...  10.9 us
    all_to_all x1, starting transfers between devices, shards(): lax.all_to_all(slot_layout(back, slots, width), 'expert', split_axis=1, c...  7.69 us
    all_to_all x1, starting transfers between devices, shards(): lax.all_to_all(fwd_send, 'expert', split_axis=1, concat_axis=1, tiled=True)  5.61 us
    all_to_all x1, starting transfers between devices, shards(): lax.all_to_all(grad_send, 'expert', split_axis=1, concat_axis=1, tiled=True)  5.41 us
  transfers between devices with their start and end apart: 7, of which 5 were waited for; matrix products, arithmetic and copies ran while one was open for 22% of the time, Pallas kernels for 0%

commit v1 on v0

v1 whole, which is shorter than its diff:
```python
import jax
import jax.numpy as jnp
from jax import lax
from jax.experimental import pallas as pl
from jax.experimental.pallas import tpu as pltpu
from jax.sharding import PartitionSpec as P

MESH = pl.DeviceIdType.MESH
BF16 = jnp.bfloat16
F32 = jnp.float32

TOP = 8
E_WIN = 4
Z = 8
Y = 8
TOK = 192
DS = 256
CAP = 12
PAD = 16
SLOTS = E_WIN * PAD
ROWS = E_WIN * CAP
HID = 128
HALF = Z * DS
X, G, B = 1, 2, 0


def dot_nt(a, b):
    return lax.dot_general(a, b, (((1,), (1,)), ((), ())), preferred_element_type=F32)


def dot_nn(a, b):
    return lax.dot_general(a, b, (((1,), (0,)), ((), ())), preferred_element_type=F32)


def dot_tn(a, b):
    return lax.dot_general(a, b, (((0,), (0,)), ((), ())), preferred_element_type=F32)


def own_tokens(whole, group):
    block = whole[:, 0:TOK]
    for g in range(1, E_WIN):
        block = jnp.where(group == g, whole[:, g * TOK : (g + 1) * TOK], block)
    return block


def pickers(routes, probs, group, before_ref):
    routes = own_tokens(routes, group)
    probs = own_tokens(probs, group)
    slot = lax.broadcasted_iota(jnp.int32, (SLOTS, TOK), 0)
    expert = slot // PAD
    chosen = jnp.zeros((SLOTS, TOK), F32)
    weight = jnp.zeros((SLOTS, TOK), F32)
    for e in range(E_WIN):
        hit = routes == e
        named = jnp.sum(jnp.where(hit, 1.0, 0.0), axis=0, keepdims=True)
        gain = jnp.sum(jnp.where(hit, probs, 0.0), axis=0, keepdims=True)
        chosen = jnp.where(expert == e, jnp.broadcast_to(named, (SLOTS, TOK)), chosen)
        weight = jnp.where(expert == e, jnp.broadcast_to(gain, (SLOTS, TOK)), weight)
    before = dot_nn(chosen.astype(BF16), before_ref[...])
    place = (slot - expert * PAD).astype(F32)
    mask = (before == place) & (chosen > 0.5)
    picker = jnp.where(mask, 1.0, 0.0).astype(BF16)
    column = jnp.sum(jnp.where(mask, weight, 0.0), axis=1, keepdims=True)
    return picker, column


def kernel(
    acts,
    grads,
    saved,
    f_routes,
    f_probs,
    b_routes,
    b_probs,
    w_gate,
    w_up,
    w_down,
    out,
    out_grads,
    relay,
    kept,
    routes,
    probs,
    wgu,
    wd,
    earlier,
    pick,
    ex,
    rows,
    ring_out,
    ring_in,
    fin,
    comb,
    local_sem,
    relay_sem,
    ex_send,
    ex_recv,
    ag_send,
    ag_recv,
    rs_send,
    rs_recv,
    fin_send,
    fin_recv,
):
    me = lax.axis_index("expert")
    section = lax.axis_index("section")
    sections = lax.axis_size("section")
    y = me // Z
    z = me % Z
    g = y // 2
    r = y % 2
    up = y * Z + (z + 1) % Z
    down = y * Z + (z + Z - 1) % Z
    after = (section + 1) % sections
    behind = (section + sections - 1) % sections
    columns = [((y + d) % Y) * Z + z for d in range(Y)]

    barrier = pltpu.get_barrier_semaphore()
    for d in (4, 3, 5, 2, 6, 1, 7):
        pl.semaphore_signal(barrier, inc=1, device_id={"expert": columns[d]}, device_id_type=MESH)
    for peer in (up, down):
        pl.semaphore_signal(barrier, inc=1, device_id={"expert": peer}, device_id_type=MESH)
    for peer in (after, behind):
        pl.semaphore_signal(barrier, inc=1, device_id={"section": peer}, device_id_type=MESH)

    loads = [
        pltpu.make_async_copy(b_routes, routes.at[1], local_sem.at[0]),
        pltpu.make_async_copy(b_probs, probs.at[1], local_sem.at[1]),
        pltpu.make_async_copy(saved, kept, local_sem.at[2]),
        pltpu.make_async_copy(f_routes, routes.at[0], local_sem.at[3]),
        pltpu.make_async_copy(f_probs, probs.at[0], local_sem.at[4]),
        pltpu.make_async_copy(w_gate, wgu.at[pl.ds(0, HID)], local_sem.at[5]),
        pltpu.make_async_copy(w_up, wgu.at[pl.ds(HID, HID)], local_sem.at[6]),
        pltpu.make_async_copy(w_down, wd, local_sem.at[7]),
    ]
    for load in loads:
        load.start()

    t0 = lax.broadcasted_iota(jnp.int32, (TOK, TOK), 0)
    t1 = lax.broadcasted_iota(jnp.int32, (TOK, TOK), 1)
    earlier[...] = jnp.where(t0 < t1, 1.0, 0.0).astype(BF16)
    slot = lax.broadcasted_iota(jnp.int32, (ROWS, SLOTS), 1)
    row = lax.broadcasted_iota(jnp.int32, (ROWS, SLOTS), 0)
    packer = jnp.where(row == (slot // PAD) * CAP + slot % PAD, jnp.where(slot % PAD < CAP, 1.0, 0.0), 0.0).astype(BF16)
    wide = lax.broadcasted_iota(jnp.int32, (SLOTS, ROWS), 0)
    long = lax.broadcasted_iota(jnp.int32, (SLOTS, ROWS), 1)
    unpacker = jnp.where(long == (wide // PAD) * CAP + wide % PAD, jnp.where(wide % PAD < CAP, 1.0, 0.0), 0.0).astype(BF16)

    def expert_slots(e):
        return pl.ds(pl.multiple_of(e * PAD, PAD), PAD)

    ex_copies = {}

    def exchange(d):
        ex[d, r, expert_slots(g), :] = pick[d, expert_slots(g), :]
        for s in (4, 3, 5, 2, 6, 1, 7):
            ex_copies[d, s] = pltpu.make_async_remote_copy(
                src_ref=pick.at[d, expert_slots(((y + s) % Y) // 2)],
                dst_ref=ex.at[d, r, expert_slots(g)],
                send_sem=ex_send.at[d, s],
                recv_sem=ex_recv.at[d, s],
                device_id={"expert": columns[s]},
                device_id_type=MESH,
            )
            ex_copies[d, s].start()

    def gather_own(d):
        for s in (1, 7, 2, 6, 3, 5, 4):
            ex_copies[d, s].wait_recv()
        for half in range(2):
            rows[d, z, half] = dot_nn(packer, ex[d, half]).astype(BF16)

    ag_copies = {}

    def pass_on(d, hop):
        for way in range(2):
            block = (z + Z - hop) % Z if way == 0 else (z + hop) % Z
            part = rows.at[d, block] if hop < 3 else rows.at[d, block, way]
            ag_copies[d, way, hop] = pltpu.make_async_remote_copy(
                src_ref=part,
                dst_ref=part,
                send_sem=ag_send.at[d, way, hop],
                recv_sem=ag_recv.at[d, way, hop],
                device_id={"expert": up if way == 0 else down},
                device_id_type=MESH,
            )
            ag_copies[d, way, hop].start()

    def arrived(d, hop):
        for way in range(2):
            ag_copies[d, way, hop].wait_recv()

    def features(block, half):
        return pl.ds(pl.multiple_of(half * HALF + block * DS, DS), DS)

    def into(d, block, total):
        for half in range(2):
            weights = wd if d == G else wgu
            term = dot_nt(rows[d, block, half], weights[:, features(block, half)])
            total = term if total is None else total + term
        return total

    totals = {B: None, X: None, G: None}

    def absorb(d, hop):
        if hop < 0:
            blocks = (z,)
        elif hop < 3:
            blocks = ((z + Z - hop - 1) % Z, (z + hop + 1) % Z)
        else:
            blocks = ((z + 4) % Z,)
        for block in blocks:
            totals[d] = into(d, block, totals[d])

    for load in loads[:3]:
        load.wait()
    b_picker, b_column = pickers(routes[1], probs[1], g, earlier)
    pick[B] = dot_nn(b_picker, kept[...]).astype(BF16)

    pl.semaphore_wait(barrier, 11)

    relays = [
        pltpu.make_async_remote_copy(
            src_ref=source,
            dst_ref=relay.at[i],
            send_sem=relay_sem.at[i],
            recv_sem=relay_sem.at[2 + i],
            device_id={"section": peer},
            device_id_type=MESH,
        )
        for i, (source, peer) in enumerate(((acts, after), (grads, behind)))
    ]
    for copy in relays:
        copy.start()
    exchange(B)

    for load in loads[3:5]:
        load.wait()
    f_picker, f_column = pickers(routes[0], probs[0], g, earlier)

    relays[0].wait_recv()
    pick[X] = dot_nn(f_picker, relay[0]).astype(BF16)
    exchange(X)
    relays[1].wait_recv()
    pick[G] = (dot_nn(b_picker, relay[1]) * b_column).astype(BF16)
    exchange(G)

    for load in loads[5:]:
        load.wait()

    gather_own(B)
    pass_on(B, 0)
    absorb(B, -1)
    gather_own(X)
    pass_on(X, 0)
    absorb(X, -1)
    arrived(B, 0)
    pass_on(B, 1)
    gather_own(G)
    pass_on(G, 0)
    absorb(B, 0)
    absorb(G, -1)
    for d, hop in ((X, 0), (B, 1), (G, 0), (X, 1), (B, 2), (G, 1), (X, 2)):
        arrived(d, hop)
        pass_on(d, hop + 1)
        absorb(d, hop)
    arrived(B, 3)
    absorb(B, 3)
    arrived(G, 2)
    pass_on(G, 3)
    absorb(G, 2)

    rs_copies = {}

    def own_part(c, block, half):
        if c == 0:
            return dot_nn(made[0], wd[:, features(block, half)])
        return dot_nn(made[1], wgu[:, features(block, half)])

    def reduce_step(c, step):
        for way in range(2):
            block = (z + 4 - step) % Z if way == 0 else (z + 4 + step) % Z
            if step > 0:
                rs_copies[c, way, step - 1].wait_recv()
            for half in range(2):
                if step == 0 and half != way:
                    continue
                value = own_part(c, block, half)
                if step > 1 or (step == 1 and half == way):
                    value = value + ring_in[c, way, step - 1, half].astype(F32)
                ring_out[c, way, step, half] = value.astype(BF16)
            at = (c, way, step) if step > 0 else (c, way, step, way)
            rs_copies[c, way, step] = pltpu.make_async_remote_copy(
                src_ref=ring_out.at[at],
                dst_ref=ring_in.at[at],
                send_sem=rs_send.at[c, way, step],
                recv_sem=rs_recv.at[c, way, step],
                device_id={"expert": up if way == 0 else down},
                device_id_type=MESH,
            )
            rs_copies[c, way, step].start()

    fin_copies = {}

    def send_back(c):
        for way in range(2):
            rs_copies[c, way, 3].wait_recv()
        for half in range(2):
            value = own_part(c, z, half)
            for way in range(2):
                value = value + ring_in[c, way, 3, half].astype(F32)
            fin[c, half] = dot_nn(unpacker, value.astype(BF16)).astype(BF16)
        comb[c, r, expert_slots(g), :] = fin[c, r, expert_slots(g), :]
        for s in (4, 3, 5, 2, 6, 1, 7):
            to = (y + s) % Y
            fin_copies[c, s] = pltpu.make_async_remote_copy(
                src_ref=fin.at[c, to % 2, expert_slots(to // 2)],
                dst_ref=comb.at[c, r, expert_slots(g)],
                send_sem=fin_send.at[c, s],
                recv_sem=fin_recv.at[c, s],
                device_id={"expert": columns[s]},
                device_id_type=MESH,
            )
            fin_copies[c, s].start()

    def place(picker, values):
        high = values.astype(BF16)
        low = (values - high.astype(F32)).astype(BF16)
        return dot_tn(picker, high) + dot_tn(picker, low)

    def finish(c, picker, column, base, target):
        for s in (1, 7, 2, 6, 3, 5, 4):
            fin_copies[c, s].wait_recv()
        values = comb[c, 0].astype(F32) + comb[c, 1].astype(F32)
        if column is not None:
            values = values * column
        target[...] = (base.astype(F32) + place(picker, values)).astype(BF16)

    made = {}

    arrived(X, 3)
    absorb(X, 3)
    gate, upper = totals[X][:, :HID], totals[X][:, HID:]
    made[0] = (gate * jax.nn.sigmoid(gate) * upper).astype(BF16)
    reduce_step(0, 0)

    gate, upper = totals[B][:, :HID], totals[B][:, HID:]
    sig = jax.nn.sigmoid(gate)
    act = gate * sig
    slope = upper * sig * (1.0 + gate * (1.0 - sig))
    arrived(G, 3)
    absorb(G, 3)
    d_hidden = totals[G]
    made[1] = jnp.concatenate([(d_hidden * slope).astype(BF16), (d_hidden * act).astype(BF16)], axis=1)
    reduce_step(1, 0)
    for step in range(1, 4):
        reduce_step(0, step)
        reduce_step(1, step)
    send_back(0)
    send_back(1)
    finish(0, f_picker, f_column, relay[0], out)
    finish(1, b_picker, None, relay[1], out_grads)

    for copies in (relays, ex_copies.values(), ag_copies.values(), rs_copies.values(), fin_copies.values()):
        for copy in copies:
            copy.wait_send()


def tick(section_acts, section_input_gradients, saved_input, fwd_routes, fwd_probs, back_routes, back_probs, w_gate, w_up, w_down):
    anywhere = pl.BlockSpec(memory_space=pl.ANY)
    inside = pl.BlockSpec(memory_space=pltpu.VMEM)
    block = jax.ShapeDtypeStruct((TOK, DS), BF16)
    dma = pltpu.SemaphoreType.DMA
    out, out_grads = pl.pallas_call(
        kernel,
        out_shape=(block, block),
        in_specs=[anywhere] * 10,
        out_specs=(inside, inside),
        scratch_shapes=[
            pltpu.VMEM((2, TOK, DS), BF16),
            pltpu.VMEM((TOK, DS), BF16),
            pltpu.VMEM((2, TOP, E_WIN * TOK), jnp.int32),
            pltpu.VMEM((2, TOP, E_WIN * TOK), F32),
            pltpu.VMEM((2 * HID, 2 * HALF), BF16),
            pltpu.VMEM((HID, 2 * HALF), BF16),
            pltpu.VMEM((TOK, TOK), BF16),
            pltpu.VMEM((3, SLOTS, DS), BF16),
            pltpu.VMEM((3, 2, SLOTS, DS), BF16),
            pltpu.VMEM((3, Z, 2, ROWS, DS), BF16),
            pltpu.VMEM((2, 2, 4, 2, ROWS, DS), BF16),
            pltpu.VMEM((2, 2, 4, 2, ROWS, DS), BF16),
            pltpu.VMEM((2, 2, SLOTS, DS), BF16),
            pltpu.VMEM((2, 2, SLOTS, DS), BF16),
            dma((8,)),
            dma((4,)),
            dma((3, Y)),
            dma((3, Y)),
            dma((3, 2, 4)),
            dma((3, 2, 4)),
            dma((2, 2, 4)),
            dma((2, 2, 4)),
            dma((2, Y)),
            dma((2, Y)),
        ],
        compiler_params=pltpu.CompilerParams(collective_id=0, has_side_effects=True),
    )(
        section_acts[0],
        section_input_gradients[0],
        saved_input[0],
        fwd_routes[0].T,
        fwd_probs[0].T,
        back_routes[0].T,
        back_probs[0].T,
        w_gate[0],
        w_up[0],
        w_down[0],
    )
    return out[None], out_grads[None]


def solution(mesh):
    spread = P("section", "expert", None)
    whole = P("section", None, None)
    return jax.shard_map(
        tick,
        mesh=mesh,
        in_specs=(spread, spread, spread, whole, whole, whole, whole, spread, spread, spread),
        out_specs=(spread, spread),
        check_vma=False,
    )
```

time: 151 us -> 70 us (0.46); the launches traced: 149 us -> 69.8 us
  Pallas kernels: 0 us -> 67 us
  waiting for transfers between devices: 62.1 us -> 0 us
  starting transfers between devices: 48.3 us -> 0 us
  local copies, waits for them, and re-layouts: 19.7 us -> 2.22 us
  matrix products: 13 us -> 0 us
  other arithmetic: 4.78 us -> 0 us
    pallas_call x0 -> x1, Pallas kernels: none -> 67 us  [tick(): pl.pallas_call(kernel, out_shape=(block, block), in_specs=[anywhere] * 10...]
    all_to_all x5 -> x0, waiting for transfers between devices: 62.1 us -> none  [the longest x1 16.8 us: shards(): lax.all_to_all(slot_layout(made, slots, width), 'expert', split_axis=1, c...]
    all_to_all x5 -> x0, starting transfers between devices: 47.4 us -> none  [the longest x1 23.5 us: shards(): lax.all_to_all(backward_outbound, 'expert', split_axis=1, concat_axis=1,...]
    dot_general x11 -> x0, matrix products: 13 us -> none  [the longest x1 2.59 us: backward_rows(): jnp.dot(d_gate, gate_w, preferred_element_type=jnp.float32)]
    reshape x8 -> x0, local copies, waits for them, and re-layouts: 7.7 us -> none  [the longest x3 4.3 us: expert_rows(): piece.reshape(count * E_WIN, piece.shape[1] * piece.shape[2] // E_WIN)]
    all_to_all x3 -> x0, local copies, waits for them, and re-layouts: 4.77 us -> none  [the longest x1 2 us: shards(): lax.all_to_all(grad_send, 'expert', split_axis=1, concat_axis=1, tiled=True)]
    broadcast_in_dim x10 -> x0, local copies, waits for them, and re-layouts: 4.64 us -> none  [the longest x9 3.25 us: fan_out(): jnp.broadcast_to(rows.reshape(capacity, E_WIN, 1, width), (capacity, E_WI...]
    another operation x4 -> x0, other arithmetic: 2.52 us -> none
  transfers between devices with their start and end apart: 7 -> 0, of which waited for: 5 -> 0; matrix products, arithmetic and copies ran while one was open for 22% -> 0% of each run, Pallas kernels for 0% -> 0%
where the time goes in v1:
time: 70 us; the launch traced here: 69.8 us
  Pallas kernels  67 us (96%)
  local copies, waits for them, and re-layouts  2.22 us (3%)
    pallas_call x1, Pallas kernels, tick(): pl.pallas_call(kernel, out_shape=(block, block), in_specs=[anywhere] * 10...  67 us
    unnamed x4, local copies, waits for them, and re-layouts  2.22 us

profile of v1, /device:TPU:14, one launch (start us, length us, event | category | flops | bytes accessed | tf_op | source)
XLA Modules:
  0.0 69.8 jit_solution(14155535820749464532)
XLA Ops:
  0.6 67.0 %shard_map.113 = (bf16[192,256]{1,0:T(8,128)(2,1)}, bf16[192,256]{1,0:T(8,128)(2,1)}) custom-call(bf16[192,256]{1,0:T(8,128)(2,1)} %bitcast.23, bf16[192,256]{1,0:T(8,128)(2,1)} %bitcast.24, bf16[192,256]{1,0:T(8,128)(2,1)} %bitcast.25, s32[8,768]{1,0:T(8,128)} %bitcast.28, f32[8,768]{1,0:T(8,128)} %bitcast.29, s32[8,768]{1,0:T(8,128)} %bitcast.30, ...), custom_call_target="tpu_custom_call" | custom-call | tf_op jit(solution)/shard_map/pallas_call | solution.py:374
  67.6 0.0 copy-start
  67.6 1.6 %copy.14 = bf16[1,192,256]{2,1,0:T(8,128)(2,1)} copy(bf16[1,192,256]{2,1,0:T(8,128)(2,1)} %bitcast.27) | data formatting | bytes 196608
  69.2 0.0 copy-done
  69.2 0.6 copy.15
Async XLA Ops:
  67.6 1.6 %copy-start = (bf16[192,256]{1,0:T(8,128)(2,1)S(1)}, bf16[192,256]{1,0:T(8,128)(2,1)}, u32[]{:S(2)}) copy-start(bf16[192,256]{1,0:T(8,128)(2,1)} %get-tuple-element.5) | copy-start | bytes 294916

commit v2 on v1

--- a/solution.py
+++ b/solution.py
@@ -22,6 +22,7 @@
 HID = 128
 HALF = Z * DS
 X, G, B = 1, 2, 0
+LONG, SHORT = 0, 4
 
 
 def dot_nt(a, b):
@@ -62,6 +63,25 @@
     picker = jnp.where(mask, 1.0, 0.0).astype(BF16)
     column = jnp.sum(jnp.where(mask, weight, 0.0), axis=1, keepdims=True)
     return picker, column
+
+
+def before_mask():
+    t0 = lax.broadcasted_iota(jnp.int32, (TOK, TOK), 0)
+    t1 = lax.broadcasted_iota(jnp.int32, (TOK, TOK), 1)
+    return jnp.where(t0 < t1, 1.0, 0.0).astype(BF16)
+
+
+def pack_matrix(shape, slot_axis):
+    slot = lax.broadcasted_iota(jnp.int32, shape, slot_axis)
+    row = lax.broadcasted_iota(jnp.int32, shape, 1 - slot_axis)
+    same = row == (slot // PAD) * CAP + slot % PAD
+    return jnp.where(same, jnp.where(slot % PAD < CAP, 1.0, 0.0), 0.0).astype(BF16)
+
+
+def identity():
+    i = lax.broadcasted_iota(jnp.int32, (SLOTS, SLOTS), 0)
+    j = lax.broadcasted_iota(jnp.int32, (SLOTS, SLOTS), 1)
+    return jnp.where(i == j, 1.0, 0.0).astype(BF16)
 
 
 def kernel(
@@ -87,10 +107,12 @@
     pick,
     ex,
     rows,
+    parts,
     ring_out,
     ring_in,
     fin,
     comb,
+    meter,
     local_sem,
     relay_sem,
     ex_send,
@@ -136,86 +158,72 @@
     for load in loads:
         load.start()
 
-    t0 = lax.broadcasted_iota(jnp.int32, (TOK, TOK), 0)
-    t1 = lax.broadcasted_iota(jnp.int32, (TOK, TOK), 1)
-    earlier[...] = jnp.where(t0 < t1, 1.0, 0.0).astype(BF16)
-    slot = lax.broadcasted_iota(jnp.int32, (ROWS, SLOTS), 1)
-    row = lax.broadcasted_iota(jnp.int32, (ROWS, SLOTS), 0)
-    packer = jnp.where(row == (slot // PAD) * CAP + slot % PAD, jnp.where(slot % PAD < CAP, 1.0, 0.0), 0.0).astype(BF16)
-    wide = lax.broadcasted_iota(jnp.int32, (SLOTS, ROWS), 0)
-    long = lax.broadcasted_iota(jnp.int32, (SLOTS, ROWS), 1)
-    unpacker = jnp.where(long == (wide // PAD) * CAP + wide % PAD, jnp.where(wide % PAD < CAP, 1.0, 0.0), 0.0).astype(BF16)
-
     def expert_slots(e):
         return pl.ds(pl.multiple_of(e * PAD, PAD), PAD)
 
-    ex_copies = {}
+    def all_of(like, sem):
+        pltpu.make_async_copy(like, like, sem).wait()
+
 
     def exchange(d):
         ex[d, r, expert_slots(g), :] = pick[d, expert_slots(g), :]
         for s in (4, 3, 5, 2, 6, 1, 7):
-            ex_copies[d, s] = pltpu.make_async_remote_copy(
+            pltpu.make_async_remote_copy(
                 src_ref=pick.at[d, expert_slots(((y + s) % Y) // 2)],
                 dst_ref=ex.at[d, r, expert_slots(g)],
-                send_sem=ex_send.at[d, s],
-                recv_sem=ex_recv.at[d, s],
+                send_sem=ex_send.at[d],
+                recv_sem=ex_recv.at[d],
                 device_id={"expert": columns[s]},
                 device_id_type=MESH,
-            )
-            ex_copies[d, s].start()
+            ).start()
 
     def gather_own(d):
-        for s in (1, 7, 2, 6, 3, 5, 4):
-            ex_copies[d, s].wait_recv()
+        all_of(meter, ex_recv.at[d])
         for half in range(2):
             rows[d, z, half] = dot_nn(packer, ex[d, half]).astype(BF16)
+        pass_on(d, 0, LONG)
+        pass_on(d, 0, SHORT)
+        absorb(d, ((z, 0), (z, 1)))
 
     ag_copies = {}
 
-    def pass_on(d, hop):
+    def pass_on(d, hop, chain):
         for way in range(2):
+            half = way if chain == LONG else 1 - way
             block = (z + Z - hop) % Z if way == 0 else (z + hop) % Z
-            part = rows.at[d, block] if hop < 3 else rows.at[d, block, way]
-            ag_copies[d, way, hop] = pltpu.make_async_remote_copy(
-                src_ref=part,
-                dst_ref=part,
-                send_sem=ag_send.at[d, way, hop],
-                recv_sem=ag_recv.at[d, way, hop],
+            piece = rows.at[d, block, half]
+            copy = pltpu.make_async_remote_copy(
+                src_ref=piece,
+                dst_ref=piece,
+                send_sem=ag_send.at[d],
+                recv_sem=ag_recv.at[d, way, chain + hop],
                 device_id={"expert": up if way == 0 else down},
                 device_id_type=MESH,
             )
-            ag_copies[d, way, hop].start()
-
-    def arrived(d, hop):
-        for way in range(2):
-            ag_copies[d, way, hop].wait_recv()
+            if hop > 0:
+                ag_copies[d, way, hop - 1, chain].wait_recv()
+            ag_copies[d, way, hop, chain] = copy
+            copy.start()
 
     def features(block, half):
         return pl.ds(pl.multiple_of(half * HALF + block * DS, DS), DS)
 
-    def into(d, block, total):
-        for half in range(2):
+    totals = {B: None, X: None, G: None}
+
+    def absorb(d, blocks):
+        for block, half in blocks:
             weights = wd if d == G else wgu
             term = dot_nt(rows[d, block, half], weights[:, features(block, half)])
-            total = term if total is None else total + term
-        return total
-
-    totals = {B: None, X: None, G: None}
-
-    def absorb(d, hop):
-        if hop < 0:
-            blocks = (z,)
-        elif hop < 3:
-            blocks = ((z + Z - hop - 1) % Z, (z + hop + 1) % Z)
+            totals[d] = term if totals[d] is None else totals[d] + term
+
+    def arrived(d, hop, chain):
+        if hop + 1 < (4 if chain == LONG else 3):
+            pass_on(d, hop + 1, chain)
         else:
-            blocks = ((z + 4) % Z,)
-        for block in blocks:
-            totals[d] = into(d, block, totals[d])
-
-    for load in loads[:3]:
-        load.wait()
-    b_picker, b_column = pickers(routes[1], probs[1], g, earlier)
-    pick[B] = dot_nn(b_picker, kept[...]).astype(BF16)
+            for way in range(2):
+                ag_copies[d, way, hop, chain].wait_recv()
+        first, second = (0, 1) if chain == LONG else (1, 0)
+        absorb(d, (((z + Z - hop - 1) % Z, first), ((z + hop + 1) % Z, second)))
 
     pl.semaphore_wait(barrier, 11)
 
@@ -232,8 +240,14 @@
     ]
     for copy in relays:
         copy.start()
+
+    earlier[...] = before_mask()
+    for load in loads[:2]:
+        load.wait()
+    b_picker, b_column = pickers(routes[1], probs[1], g, earlier)
+    loads[2].wait()
+    pick[B] = dot_nn(b_picker, kept[...]).astype(BF16)
     exchange(B)
-
     for load in loads[3:5]:
         load.wait()
     f_picker, f_column = pickers(routes[0], probs[0], g, earlier)
@@ -245,30 +259,24 @@
     pick[G] = (dot_nn(b_picker, relay[1]) * b_column).astype(BF16)
     exchange(G)
 
+    packer = pack_matrix((ROWS, SLOTS), 1)
+    unpacker = pack_matrix((SLOTS, ROWS), 0)
+    token_of = [dot_tn(p, identity()).astype(BF16) for p in (f_picker, b_picker)]
+
     for load in loads[5:]:
         load.wait()
 
     gather_own(B)
-    pass_on(B, 0)
-    absorb(B, -1)
     gather_own(X)
-    pass_on(X, 0)
-    absorb(X, -1)
-    arrived(B, 0)
-    pass_on(B, 1)
+    arrived(B, 0, LONG)
+    arrived(B, 0, SHORT)
     gather_own(G)
-    pass_on(G, 0)
-    absorb(B, 0)
-    absorb(G, -1)
     for d, hop in ((X, 0), (B, 1), (G, 0), (X, 1), (B, 2), (G, 1), (X, 2)):
-        arrived(d, hop)
-        pass_on(d, hop + 1)
-        absorb(d, hop)
-    arrived(B, 3)
-    absorb(B, 3)
-    arrived(G, 2)
-    pass_on(G, 3)
-    absorb(G, 2)
+        arrived(d, hop, LONG)
+        arrived(d, hop, SHORT)
+    arrived(B, 3, LONG)
+    arrived(G, 2, LONG)
+    arrived(G, 2, SHORT)
 
     rs_copies = {}
 
@@ -277,60 +285,64 @@
             return dot_nn(made[0], wd[:, features(block, half)])
         return dot_nn(made[1], wgu[:, features(block, half)])
 
-    def reduce_step(c, step):
+    def turns(turn):
         for way in range(2):
+            yield way, way, turn
+        if turn < 3:
+            for way in range(2):
+                yield way, 1 - way, turn + 1
+
+    def own_parts(c, turn):
+        for way, half, step in turns(turn):
             block = (z + 4 - step) % Z if way == 0 else (z + 4 + step) % Z
-            if step > 0:
-                rs_copies[c, way, step - 1].wait_recv()
-            for half in range(2):
-                if step == 0 and half != way:
-                    continue
-                value = own_part(c, block, half)
-                if step > 1 or (step == 1 and half == way):
-                    value = value + ring_in[c, way, step - 1, half].astype(F32)
-                ring_out[c, way, step, half] = value.astype(BF16)
-            at = (c, way, step) if step > 0 else (c, way, step, way)
-            rs_copies[c, way, step] = pltpu.make_async_remote_copy(
+            parts[c, way, step, half] = own_part(c, block, half)
+
+    def reduce_turn(c, turn):
+        for way, half, step in turns(turn):
+            value = parts[c, way, step, half]
+            if turn > 0:
+                rs_copies[c, way, half, turn - 1].wait_recv()
+                value = value + ring_in[c, way, step - 1, half].astype(F32)
+            ring_out[c, way, step, half] = value.astype(BF16)
+            at = (c, way, step, half)
+            copy = pltpu.make_async_remote_copy(
                 src_ref=ring_out.at[at],
                 dst_ref=ring_in.at[at],
-                send_sem=rs_send.at[c, way, step],
-                recv_sem=rs_recv.at[c, way, step],
+                send_sem=rs_send.at[c],
+                recv_sem=rs_recv.at[c, way, (LONG if half == way else SHORT) + turn],
                 device_id={"expert": up if way == 0 else down},
                 device_id_type=MESH,
             )
-            rs_copies[c, way, step].start()
-
-    fin_copies = {}
+            rs_copies[c, way, half, turn] = copy
+            copy.start()
 
     def send_back(c):
-        for way in range(2):
-            rs_copies[c, way, 3].wait_recv()
+        mine = [own_part(c, z, half) for half in range(2)]
         for half in range(2):
-            value = own_part(c, z, half)
-            for way in range(2):
+            value = mine[half]
+            for way in (1 - half, half):
+                rs_copies[c, way, half, 3 if half == way else 2].wait_recv()
                 value = value + ring_in[c, way, 3, half].astype(F32)
             fin[c, half] = dot_nn(unpacker, value.astype(BF16)).astype(BF16)
         comb[c, r, expert_slots(g), :] = fin[c, r, expert_slots(g), :]
         for s in (4, 3, 5, 2, 6, 1, 7):
             to = (y + s) % Y
-            fin_copies[c, s] = pltpu.make_async_remote_copy(
+            pltpu.make_async_remote_copy(
                 src_ref=fin.at[c, to % 2, expert_slots(to // 2)],
                 dst_ref=comb.at[c, r, expert_slots(g)],
-                send_sem=fin_send.at[c, s],
-                recv_sem=fin_recv.at[c, s],
+                send_sem=fin_send.at[c],
+                recv_sem=fin_recv.at[c],
                 device_id={"expert": columns[s]},
                 device_id_type=MESH,
-            )
-            fin_copies[c, s].start()
+            ).start()
 
     def place(picker, values):
         high = values.astype(BF16)
         low = (values - high.astype(F32)).astype(BF16)
-        return dot_tn(picker, high) + dot_tn(picker, low)
+        return dot_nn(picker, high) + dot_nn(picker, low)
 
     def finish(c, picker, column, base, target):
-        for s in (1, 7, 2, 6, 3, 5, 4):
-            fin_copies[c, s].wait_recv()
+        all_of(meter, fin_recv.at[c])
         values = comb[c, 0].astype(F32) + comb[c, 1].astype(F32)
         if column is not None:
             values = values * column
@@ -338,38 +350,47 @@
 
     made = {}
 
-    arrived(X, 3)
-    absorb(X, 3)
+    arrived(X, 3, LONG)
     gate, upper = totals[X][:, :HID], totals[X][:, HID:]
     made[0] = (gate * jax.nn.sigmoid(gate) * upper).astype(BF16)
-    reduce_step(0, 0)
+    own_parts(0, 0)
+    reduce_turn(0, 0)
 
     gate, upper = totals[B][:, :HID], totals[B][:, HID:]
     sig = jax.nn.sigmoid(gate)
     act = gate * sig
     slope = upper * sig * (1.0 + gate * (1.0 - sig))
-    arrived(G, 3)
-    absorb(G, 3)
+    arrived(G, 3, LONG)
     d_hidden = totals[G]
     made[1] = jnp.concatenate([(d_hidden * slope).astype(BF16), (d_hidden * act).astype(BF16)], axis=1)
-    reduce_step(1, 0)
-    for step in range(1, 4):
-        reduce_step(0, step)
-        reduce_step(1, step)
+    own_parts(1, 0)
+    reduce_turn(1, 0)
+    for turn in range(1, 4):
+        for c in range(2):
+            own_parts(c, turn)
+            reduce_turn(c, turn)
     send_back(0)
     send_back(1)
-    finish(0, f_picker, f_column, relay[0], out)
-    finish(1, b_picker, None, relay[1], out_grads)
-
-    for copies in (relays, ex_copies.values(), ag_copies.values(), rs_copies.values(), fin_copies.values()):
-        for copy in copies:
+    finish(0, token_of[0], f_column, relay[0], out)
+    finish(1, token_of[1], None, relay[1], out_grads)
+
+    def drain():
+        for copy in relays:
             copy.wait_send()
+        for d in range(3):
+            all_of(meter, ex_send.at[d])
+            all_of(rows.at[d, pl.ds(0, 7)], ag_send.at[d])
+        for c in range(2):
+            all_of(rows.at[c, pl.ds(0, 7)], rs_send.at[c])
+            all_of(meter, fin_send.at[c])
+
+    drain()
 
 
 def tick(section_acts, section_input_gradients, saved_input, fwd_routes, fwd_probs, back_routes, back_probs, w_gate, w_up, w_down):
     anywhere = pl.BlockSpec(memory_space=pl.ANY)
     inside = pl.BlockSpec(memory_space=pltpu.VMEM)
-    block = jax.ShapeDtypeStruct((TOK, DS), BF16)
+    block = pltpu.VMEM((TOK, DS), BF16)
     dma = pltpu.SemaphoreType.DMA
     out, out_grads = pl.pallas_call(
         kernel,
@@ -387,20 +408,22 @@
             pltpu.VMEM((3, SLOTS, DS), BF16),
             pltpu.VMEM((3, 2, SLOTS, DS), BF16),
             pltpu.VMEM((3, Z, 2, ROWS, DS), BF16),
+            pltpu.VMEM((2, 2, 4, 2, ROWS, DS), F32),
             pltpu.VMEM((2, 2, 4, 2, ROWS, DS), BF16),
             pltpu.VMEM((2, 2, 4, 2, ROWS, DS), BF16),
             pltpu.VMEM((2, 2, SLOTS, DS), BF16),
             pltpu.VMEM((2, 2, SLOTS, DS), BF16),
+            pltpu.VMEM((7, PAD, DS), BF16),
             dma((8,)),
             dma((4,)),
-            dma((3, Y)),
-            dma((3, Y)),
-            dma((3, 2, 4)),
-            dma((3, 2, 4)),
-            dma((2, 2, 4)),
-            dma((2, 2, 4)),
-            dma((2, Y)),
-            dma((2, Y)),
+            dma((3,)),
+            dma((3,)),
+            dma((3,)),
+            dma((3, 2, 7)),
+            dma((2,)),
+            dma((2, 2, 7)),
+            dma((2,)),
+            dma((2,)),
         ],
         compiler_params=pltpu.CompilerParams(collective_id=0, has_side_effects=True),
     )(

time: 70 us -> 65.5 us (0.936)
  Pallas kernels: 67 us -> 63 us
  local copies, waits for them, and re-layouts: 2.22 us -> 1.28 us
    pallas_call x1, Pallas kernels: 67 us -> 63 us  [tick(): pl.pallas_call(kernel, out_shape=(block, block), in_specs=[anywhere] * 10...]
    unnamed x4 -> x2, local copies, waits for them, and re-layouts: 2.22 us -> 1.28 us
where the time goes in v2:
time: 65.5 us; the launch traced here: 65 us
  Pallas kernels  63 us (96%)
  local copies, waits for them, and re-layouts  1.28 us (2%)
    pallas_call x1, Pallas kernels, tick(): pl.pallas_call(kernel, out_shape=(block, block), in_specs=[anywhere] * 10...  63 us

profile of v2, /device:TPU:14, one launch (start us, length us, event | category | flops | bytes accessed | tf_op | source)
XLA Modules:
  0.0 65.0 jit_solution(8946010020796094201)
XLA Ops:
  0.6 63.0 %shard_map.113 = (bf16[192,256]{1,0:T(8,128)(2,1)S(1)}, bf16[192,256]{1,0:T(8,128)(2,1)S(1)}) custom-call(bf16[192,256]{1,0:T(8,128)(2,1)} %bitcast.25, bf16[192,256]{1,0:T(8,128)(2,1)} %bitcast.26, bf16[192,256]{1,0:T(8,128)(2,1)} %bitcast.27, s32[8,768]{1,0:T(8,128)} %bitcast.28, f32[8,768]{1,0:T(8,128)} %bitcast.29, s32[8,768]{1,0:T(8,128)} %bitcast.30, ...), custom_call_target="tpu_custom_call" | custom-call | tf_op jit(solution)/shard_map/pallas_call | solution.py:395
  63.7 0.6 copy.14
  64.3 0.6 copy.15

commit v3 on v2

--- a/solution.py
+++ b/solution.py
@@ -23,6 +23,7 @@
 HALF = Z * DS
 X, G, B = 1, 2, 0
 LONG, SHORT = 0, 4
+DIRECT = (G,)
 
 
 def dot_nt(a, b):
@@ -115,13 +116,12 @@
     meter,
     local_sem,
     relay_sem,
-    ex_send,
+    small_send,
     ex_recv,
     ag_send,
     ag_recv,
     rs_send,
     rs_recv,
-    fin_send,
     fin_recv,
 ):
     me = lax.axis_index("expert")
@@ -133,6 +133,8 @@
     r = y % 2
     up = y * Z + (z + 1) % Z
     down = y * Z + (z + Z - 1) % Z
+    up_two = y * Z + (z + 2) % Z
+    down_two = y * Z + (z + Z - 2) % Z
     after = (section + 1) % sections
     behind = (section + sections - 1) % sections
     columns = [((y + d) % Y) * Z + z for d in range(Y)]
@@ -140,20 +142,20 @@
     barrier = pltpu.get_barrier_semaphore()
     for d in (4, 3, 5, 2, 6, 1, 7):
         pl.semaphore_signal(barrier, inc=1, device_id={"expert": columns[d]}, device_id_type=MESH)
-    for peer in (up, down):
+    for peer in (up, down, up_two, down_two):
         pl.semaphore_signal(barrier, inc=1, device_id={"expert": peer}, device_id_type=MESH)
     for peer in (after, behind):
         pl.semaphore_signal(barrier, inc=1, device_id={"section": peer}, device_id_type=MESH)
 
     loads = [
         pltpu.make_async_copy(b_routes, routes.at[1], local_sem.at[0]),
-        pltpu.make_async_copy(b_probs, probs.at[1], local_sem.at[1]),
-        pltpu.make_async_copy(saved, kept, local_sem.at[2]),
-        pltpu.make_async_copy(f_routes, routes.at[0], local_sem.at[3]),
-        pltpu.make_async_copy(f_probs, probs.at[0], local_sem.at[4]),
-        pltpu.make_async_copy(w_gate, wgu.at[pl.ds(0, HID)], local_sem.at[5]),
-        pltpu.make_async_copy(w_up, wgu.at[pl.ds(HID, HID)], local_sem.at[6]),
-        pltpu.make_async_copy(w_down, wd, local_sem.at[7]),
+        pltpu.make_async_copy(b_probs, probs.at[1], local_sem.at[0]),
+        pltpu.make_async_copy(saved, kept, local_sem.at[1]),
+        pltpu.make_async_copy(f_routes, routes.at[0], local_sem.at[2]),
+        pltpu.make_async_copy(f_probs, probs.at[0], local_sem.at[2]),
+        pltpu.make_async_copy(w_gate, wgu.at[pl.ds(0, HID)], local_sem.at[3]),
+        pltpu.make_async_copy(w_up, wgu.at[pl.ds(HID, HID)], local_sem.at[3]),
+        pltpu.make_async_copy(w_down, wd, local_sem.at[4]),
     ]
     for load in loads:
         load.start()
@@ -171,14 +173,14 @@
             pltpu.make_async_remote_copy(
                 src_ref=pick.at[d, expert_slots(((y + s) % Y) // 2)],
                 dst_ref=ex.at[d, r, expert_slots(g)],
-                send_sem=ex_send.at[d],
+                send_sem=small_send,
                 recv_sem=ex_recv.at[d],
                 device_id={"expert": columns[s]},
                 device_id_type=MESH,
             ).start()
 
     def gather_own(d):
-        all_of(meter, ex_recv.at[d])
+        all_of(meter.at[0], ex_recv.at[d])
         for half in range(2):
             rows[d, z, half] = dot_nn(packer, ex[d, half]).astype(BF16)
         pass_on(d, 0, LONG)
@@ -195,15 +197,31 @@
             copy = pltpu.make_async_remote_copy(
                 src_ref=piece,
                 dst_ref=piece,
-                send_sem=ag_send.at[d],
+                send_sem=ag_send,
                 recv_sem=ag_recv.at[d, way, chain + hop],
                 device_id={"expert": up if way == 0 else down},
                 device_id_type=MESH,
             )
             if hop > 0:
                 ag_copies[d, way, hop - 1, chain].wait_recv()
+            if hop == 2 and chain == LONG and d in DIRECT:
+                skip(d, way)
             ag_copies[d, way, hop, chain] = copy
             copy.start()
+
+    def skip(d, way):
+        block = (z + Z - 2) % Z if way == 0 else (z + 2) % Z
+        piece = rows.at[d, block, way]
+        copy = pltpu.make_async_remote_copy(
+            src_ref=piece,
+            dst_ref=piece,
+            send_sem=ag_send,
+            recv_sem=ag_recv.at[d, way, LONG + 3],
+            device_id={"expert": up_two if way == 0 else down_two},
+            device_id_type=MESH,
+        )
+        ag_copies[d, way, 3, LONG] = copy
+        copy.start()
 
     def features(block, half):
         return pl.ds(pl.multiple_of(half * HALF + block * DS, DS), DS)
@@ -217,7 +235,7 @@
             totals[d] = term if totals[d] is None else totals[d] + term
 
     def arrived(d, hop, chain):
-        if hop + 1 < (4 if chain == LONG else 3):
+        if hop < 2 or (hop == 2 and chain == LONG and d not in DIRECT):
             pass_on(d, hop + 1, chain)
         else:
             for way in range(2):
@@ -225,7 +243,7 @@
         first, second = (0, 1) if chain == LONG else (1, 0)
         absorb(d, (((z + Z - hop - 1) % Z, first), ((z + hop + 1) % Z, second)))
 
-    pl.semaphore_wait(barrier, 11)
+    pl.semaphore_wait(barrier, 13)
 
     relays = [
         pltpu.make_async_remote_copy(
@@ -242,14 +260,12 @@
         copy.start()
 
     earlier[...] = before_mask()
-    for load in loads[:2]:
-        load.wait()
+    all_of(probs, local_sem.at[0])
     b_picker, b_column = pickers(routes[1], probs[1], g, earlier)
     loads[2].wait()
     pick[B] = dot_nn(b_picker, kept[...]).astype(BF16)
     exchange(B)
-    for load in loads[3:5]:
-        load.wait()
+    all_of(probs, local_sem.at[2])
     f_picker, f_column = pickers(routes[0], probs[0], g, earlier)
 
     relays[0].wait_recv()
@@ -263,8 +279,8 @@
     unpacker = pack_matrix((SLOTS, ROWS), 0)
     token_of = [dot_tn(p, identity()).astype(BF16) for p in (f_picker, b_picker)]
 
-    for load in loads[5:]:
-        load.wait()
+    all_of(wgu, local_sem.at[3])
+    all_of(wd, local_sem.at[4])
 
     gather_own(B)
     gather_own(X)
@@ -286,34 +302,39 @@
         return dot_nn(made[1], wgu[:, features(block, half)])
 
     def turns(turn):
-        for way in range(2):
-            yield way, way, turn
-        if turn < 3:
+        if turn == 0:
             for way in range(2):
-                yield way, 1 - way, turn + 1
+                yield way, way, 0
+        for far in (0, 1):
+            for way in range(2):
+                yield way, way if far else 1 - way, turn + 1
+
+    def part_of(way, step):
+        return (z + 4 - step) % Z if way == 0 else (z + 4 + step) % Z
 
     def own_parts(c, turn):
         for way, half, step in turns(turn):
-            block = (z + 4 - step) % Z if way == 0 else (z + 4 + step) % Z
-            parts[c, way, step, half] = own_part(c, block, half)
+            parts[c, way, step, half] = own_part(c, part_of(way, step), half)
 
     def reduce_turn(c, turn):
         for way, half, step in turns(turn):
-            value = parts[c, way, step, half]
-            if turn > 0:
-                rs_copies[c, way, half, turn - 1].wait_recv()
-                value = value + ring_in[c, way, step - 1, half].astype(F32)
+            value = parts[c, way, step, half] if turn > 0 else own_part(c, part_of(way, step), half)
+            sources = (1, 0) if step == 2 and half == way else (step - 1,) if step > 1 else ()
+            for source in sources:
+                rs_copies[c, way, half, source].wait_recv()
+                value = value + ring_in[c, way, source, half].astype(F32)
             ring_out[c, way, step, half] = value.astype(BF16)
             at = (c, way, step, half)
+            next_one, next_two = (up, up_two) if way == 0 else (down, down_two)
             copy = pltpu.make_async_remote_copy(
                 src_ref=ring_out.at[at],
                 dst_ref=ring_in.at[at],
-                send_sem=rs_send.at[c],
-                recv_sem=rs_recv.at[c, way, (LONG if half == way else SHORT) + turn],
-                device_id={"expert": up if way == 0 else down},
+                send_sem=rs_send,
+                recv_sem=rs_recv.at[c, way, step if half == way else 3 + step],
+                device_id={"expert": next_two if step == 0 else next_one},
                 device_id_type=MESH,
             )
-            rs_copies[c, way, half, turn] = copy
+            rs_copies[c, way, half, step] = copy
             copy.start()
 
     def send_back(c):
@@ -321,7 +342,7 @@
         for half in range(2):
             value = mine[half]
             for way in (1 - half, half):
-                rs_copies[c, way, half, 3 if half == way else 2].wait_recv()
+                rs_copies[c, way, half, 3].wait_recv()
                 value = value + ring_in[c, way, 3, half].astype(F32)
             fin[c, half] = dot_nn(unpacker, value.astype(BF16)).astype(BF16)
         comb[c, r, expert_slots(g), :] = fin[c, r, expert_slots(g), :]
@@ -330,7 +351,7 @@
             pltpu.make_async_remote_copy(
                 src_ref=fin.at[c, to % 2, expert_slots(to // 2)],
                 dst_ref=comb.at[c, r, expert_slots(g)],
-                send_sem=fin_send.at[c],
+                send_sem=small_send,
                 recv_sem=fin_recv.at[c],
                 device_id={"expert": columns[s]},
                 device_id_type=MESH,
@@ -342,7 +363,7 @@
         return dot_nn(picker, high) + dot_nn(picker, low)
 
     def finish(c, picker, column, base, target):
-        all_of(meter, fin_recv.at[c])
+        all_of(meter.at[0], fin_recv.at[c])
         values = comb[c, 0].astype(F32) + comb[c, 1].astype(F32)
         if column is not None:
             values = values * column
@@ -353,7 +374,6 @@
     arrived(X, 3, LONG)
     gate, upper = totals[X][:, :HID], totals[X][:, HID:]
     made[0] = (gate * jax.nn.sigmoid(gate) * upper).astype(BF16)
-    own_parts(0, 0)
     reduce_turn(0, 0)
 
     gate, upper = totals[B][:, :HID], totals[B][:, HID:]
@@ -363,9 +383,8 @@
     arrived(G, 3, LONG)
     d_hidden = totals[G]
     made[1] = jnp.concatenate([(d_hidden * slope).astype(BF16), (d_hidden * act).astype(BF16)], axis=1)
-    own_parts(1, 0)
     reduce_turn(1, 0)
-    for turn in range(1, 4):
+    for turn in range(1, 3):
         for c in range(2):
             own_parts(c, turn)
             reduce_turn(c, turn)
@@ -377,14 +396,19 @@
     def drain():
         for copy in relays:
             copy.wait_send()
-        for d in range(3):
-            all_of(meter, ex_send.at[d])
-            all_of(rows.at[d, pl.ds(0, 7)], ag_send.at[d])
-        for c in range(2):
-            all_of(rows.at[c, pl.ds(0, 7)], rs_send.at[c])
-            all_of(meter, fin_send.at[c])
+        all_of(meter, small_send)
+        all_of(rows.at[:, pl.ds(0, 7)], ag_send)
+        all_of(rows.at[pl.ds(0, 2), pl.ds(0, 7)], rs_send)
 
     drain()
+
+
+def write_out(first, second, out, out_grads, sem):
+    copies = [pltpu.make_async_copy(a, b, sem.at[i]) for i, (a, b) in enumerate(((first, out), (second, out_grads)))]
+    for copy in copies:
+        copy.start()
+    for copy in copies:
+        copy.wait()
 
 
 def tick(section_acts, section_input_gradients, saved_input, fwd_routes, fwd_probs, back_routes, back_probs, w_gate, w_up, w_down):
@@ -413,16 +437,15 @@
             pltpu.VMEM((2, 2, 4, 2, ROWS, DS), BF16),
             pltpu.VMEM((2, 2, SLOTS, DS), BF16),
             pltpu.VMEM((2, 2, SLOTS, DS), BF16),
-            pltpu.VMEM((7, PAD, DS), BF16),
-            dma((8,)),
+            pltpu.VMEM((5, 7, PAD, DS), BF16),
+            dma((5,)),
             dma((4,)),
+            dma,
             dma((3,)),
-            dma((3,)),
-            dma((3,)),
+            dma,
             dma((3, 2, 7)),
-            dma((2,)),
+            dma,
             dma((2, 2, 7)),
-            dma((2,)),
             dma((2,)),
         ],
         compiler_params=pltpu.CompilerParams(collective_id=0, has_side_effects=True),
@@ -438,6 +461,14 @@
         w_up[0],
         w_down[0],
     )
+    block = jax.ShapeDtypeStruct((TOK, DS), BF16)
+    out, out_grads = pl.pallas_call(
+        write_out,
+        out_shape=(block, block),
+        in_specs=[inside] * 2,
+        out_specs=(anywhere, anywhere),
+        scratch_shapes=[dma((2,))],
+    )(*(pltpu.with_memory_space_constraint(v, pltpu.VMEM) for v in (out, out_grads)))
     return out[None], out_grads[None]
 
 

time: 65.5 us -> 64.5 us (0.985)
  local copies, waits for them, and re-layouts: 1.28 us -> 0 us
    unnamed x2 -> x0, local copies, waits for them, and re-layouts: 1.28 us -> none
    pallas_call x1, Pallas kernels: 63 us -> 62.1 us  [tick(): pl.pallas_call(kernel, out_shape=(block, block), in_specs=[anywhere] * 10...]
    pallas_call x0 -> x1, Pallas kernels: none -> 0.69 us  [tick(): pl.pallas_call(write_out, out_shape=(block, block), in_specs=[inside] * 2...]
where the time goes in v3:
time: 64.5 us; the launch traced here: 63.4 us
  Pallas kernels  62.8 us (97%)
    pallas_call x1, Pallas kernels, tick(): pl.pallas_call(kernel, out_shape=(block, block), in_specs=[anywhere] * 10...  62.1 us

profile of v3, /device:TPU:14, one launch (start us, length us, event | category | flops | bytes accessed | tf_op | source)
XLA Modules:
  0.0 63.4 jit_solution(12230559149227574541)
XLA Ops:
  0.6 62.1 %shard_map.113 = (bf16[192,256]{1,0:T(8,128)(2,1)S(1)}, bf16[192,256]{1,0:T(8,128)(2,1)S(1)}) custom-call(bf16[192,256]{1,0:T(8,128)(2,1)} %bitcast.23, bf16[192,256]{1,0:T(8,128)(2,1)} %bitcast.24, bf16[192,256]{1,0:T(8,128)(2,1)} %bitcast.25, s32[8,768]{1,0:T(8,128)} %bitcast.26, f32[8,768]{1,0:T(8,128)} %bitcast.27, s32[8,768]{1,0:T(8,128)} %bitcast.28, ...), custom_call_target="tpu_custom_call" | custom-call | tf_op jit(solution)/shard_map/pallas_call | solution.py:419
  62.7 0.7 %shard_map.114 = (bf16[192,256]{1,0:T(8,128)(2,1)}, bf16[192,256]{1,0:T(8,128)(2,1)}) custom-call(bf16[192,256]{1,0:T(8,128)(2,1)S(1)} %get-tuple-element.6.first, bf16[192,256]{1,0:T(8,128)(2,1)S(1)} %get-tuple-element.7.second), custom_call_target="tpu_custom_call" | custom-call | tf_op jit(solution)/shard_map/pallas_call | solution.py:465

commit v4 on v3

--- a/solution.py
+++ b/solution.py
@@ -133,6 +133,7 @@
     r = y % 2
     up = y * Z + (z + 1) % Z
     down = y * Z + (z + Z - 1) % Z
+    partner = (2 * g + 1 - r) * Z + z
     up_two = y * Z + (z + 2) % Z
     down_two = y * Z + (z + Z - 2) % Z
     after = (section + 1) % sections
@@ -183,11 +184,68 @@
         all_of(meter.at[0], ex_recv.at[d])
         for half in range(2):
             rows[d, z, half] = dot_nn(packer, ex[d, half]).astype(BF16)
-        pass_on(d, 0, LONG)
-        pass_on(d, 0, SHORT)
+        if d == B:
+            own_hop(0)
+            other_hop(0)
+        else:
+            pass_on(d, 0, LONG)
+            pass_on(d, 0, SHORT)
         absorb(d, ((z, 0), (z, 1)))
 
     ag_copies = {}
+    paired = {}
+
+    def send_piece(key, block, half, peer, sem):
+        piece = rows.at[B, block, half]
+        paired[key] = pltpu.make_async_remote_copy(
+            src_ref=piece,
+            dst_ref=piece,
+            send_sem=ag_send,
+            recv_sem=ag_recv.at[B, sem // 7, sem % 7],
+            device_id={"expert": peer},
+            device_id_type=MESH,
+        )
+        paired[key].start()
+
+    def beside(way, distance):
+        return (z + Z - distance) % Z if way == 0 else (z + distance) % Z
+
+    def own_hop(hop):
+        for way in range(2):
+            if hop > 0:
+                paired["own", way, hop - 1].wait_recv()
+            if hop < 3:
+                send_piece(("own", way, hop), beside(way, hop), r, up if way == 0 else down, way * 3 + hop)
+            else:
+                send_piece(("pair", way), beside(way, 3), r, partner, 10 + way)
+        if hop == 3:
+            send_piece("far", (z + 5 + 6 * r) % Z, r, up + r * (down - up), 12)
+
+    def other_hop(hop):
+        for way in range(2):
+            if hop > 0:
+                paired["other", way, hop - 1].wait_recv()
+            if hop < 2:
+                send_piece(("other", way, hop), beside(way, hop), 1 - r, up if way == 0 else down, 6 + way * 2 + hop)
+
+    def arrived_kept(hop, chain):
+        if chain == LONG and hop < 3:
+            own_hop(hop + 1)
+            absorb(B, [(beside(way, hop + 1), r) for way in range(2)])
+        elif chain == LONG:
+            paired["far"].wait_recv()
+            send_piece("last", (z + 4) % Z, r, partner, 13)
+            absorb(B, [((z + 4) % Z, r)])
+        elif hop < 2:
+            other_hop(hop + 1)
+            absorb(B, [(beside(way, hop + 1), 1 - r) for way in range(2)])
+
+    def arrived_pair():
+        for way in range(2):
+            paired["pair", way].wait_recv()
+        absorb(B, [(beside(way, 3), 1 - r) for way in range(2)])
+        paired["last"].wait_recv()
+        absorb(B, [((z + 4) % Z, 1 - r)])
 
     def pass_on(d, hop, chain):
         for way in range(2):
@@ -235,6 +293,9 @@
             totals[d] = term if totals[d] is None else totals[d] + term
 
     def arrived(d, hop, chain):
+        if d == B:
+            arrived_kept(hop, chain)
+            return
         if hop < 2 or (hop == 2 and chain == LONG and d not in DIRECT):
             pass_on(d, hop + 1, chain)
         else:
@@ -243,6 +304,11 @@
         first, second = (0, 1) if chain == LONG else (1, 0)
         absorb(d, (((z + Z - hop - 1) % Z, first), ((z + hop + 1) % Z, second)))
 
+    earlier[...] = before_mask()
+    all_of(probs, local_sem.at[0])
+    b_picker, b_column = pickers(routes[1], probs[1], g, earlier)
+    loads[2].wait()
+    pick[B] = dot_nn(b_picker, kept[...]).astype(BF16)
     pl.semaphore_wait(barrier, 13)
 
     relays = [
@@ -259,11 +325,6 @@
     for copy in relays:
         copy.start()
 
-    earlier[...] = before_mask()
-    all_of(probs, local_sem.at[0])
-    b_picker, b_column = pickers(routes[1], probs[1], g, earlier)
-    loads[2].wait()
-    pick[B] = dot_nn(b_picker, kept[...]).astype(BF16)
     exchange(B)
     all_of(probs, local_sem.at[2])
     f_picker, f_column = pickers(routes[0], probs[0], g, earlier)
@@ -293,6 +354,7 @@
     arrived(B, 3, LONG)
     arrived(G, 2, LONG)
     arrived(G, 2, SHORT)
+    arrived_pair()
 
     rs_copies = {}
 

time: 64.5 us -> 63.6 us (0.986)
  no operation moved by 1% of the time
where the time goes in v4:
time: 63.6 us; the launch traced here: 62.8 us
  Pallas kernels  62.2 us (98%)
  between operations  0.64 us (1%)
    pallas_call x1, Pallas kernels, tick(): pl.pallas_call(kernel, out_shape=(block, block), in_specs=[anywhere] * 10...  61.5 us

profile of v4, /device:TPU:14, one launch (start us, length us, event | category | flops | bytes accessed | tf_op | source)
XLA Modules:
  0.0 62.8 jit_solution(6473297483832087210)
XLA Ops:
  0.6 61.5 %shard_map.113 = (bf16[192,256]{1,0:T(8,128)(2,1)S(1)}, bf16[192,256]{1,0:T(8,128)(2,1)S(1)}) custom-call(bf16[192,256]{1,0:T(8,128)(2,1)} %bitcast.23, bf16[192,256]{1,0:T(8,128)(2,1)} %bitcast.24, bf16[192,256]{1,0:T(8,128)(2,1)} %bitcast.25, s32[8,768]{1,0:T(8,128)} %bitcast.26, f32[8,768]{1,0:T(8,128)} %bitcast.27, s32[8,768]{1,0:T(8,128)} %bitcast.28, ...), custom_call_target="tpu_custom_call" | custom-call | tf_op jit(solution)/shard_map/pallas_call | solution.py:481
  62.1 0.7 %shard_map.114 = (bf16[192,256]{1,0:T(8,128)(2,1)}, bf16[192,256]{1,0:T(8,128)(2,1)}) custom-call(bf16[192,256]{1,0:T(8,128)(2,1)S(1)} %get-tuple-element.6.first, bf16[192,256]{1,0:T(8,128)(2,1)S(1)} %get-tuple-element.7.second), custom_call_target="tpu_custom_call" | custom-call | tf_op jit(solution)/shard_map/pallas_call | solution.py:527

commit v5 on v4

--- a/solution.py
+++ b/solution.py
@@ -354,7 +354,6 @@
     arrived(B, 3, LONG)
     arrived(G, 2, LONG)
     arrived(G, 2, SHORT)
-    arrived_pair()
 
     rs_copies = {}
 
@@ -437,6 +436,7 @@
     gate, upper = totals[X][:, :HID], totals[X][:, HID:]
     made[0] = (gate * jax.nn.sigmoid(gate) * upper).astype(BF16)
     reduce_turn(0, 0)
+    arrived_pair()
 
     gate, upper = totals[B][:, :HID], totals[B][:, HID:]
     sig = jax.nn.sigmoid(gate)

time: 63.6 us -> 63.4 us (level)
  no operation moved by 1% of the time
where the time goes in v5:
time: 63.4 us; the launch traced here: 62.7 us
  Pallas kernels  62.1 us (98%)
  between operations  0.64 us (1%)
    pallas_call x1, Pallas kernels, tick(): pl.pallas_call(kernel, out_shape=(block, block), in_specs=[anywhere] * 10...  61.4 us

profile of v5, /device:TPU:14, one launch (start us, length us, event | category | flops | bytes accessed | tf_op | source)
XLA Modules:
  0.0 62.7 jit_solution(764544919163249788)
XLA Ops:
  0.6 61.4 %shard_map.113 = (bf16[192,256]{1,0:T(8,128)(2,1)S(1)}, bf16[192,256]{1,0:T(8,128)(2,1)S(1)}) custom-call(bf16[192,256]{1,0:T(8,128)(2,1)} %bitcast.23, bf16[192,256]{1,0:T(8,128)(2,1)} %bitcast.24, bf16[192,256]{1,0:T(8,128)(2,1)} %bitcast.25, s32[8,768]{1,0:T(8,128)} %bitcast.26, f32[8,768]{1,0:T(8,128)} %bitcast.27, s32[8,768]{1,0:T(8,128)} %bitcast.28, ...), custom_call_target="tpu_custom_call" | custom-call | tf_op jit(solution)/shard_map/pallas_call | solution.py:481
  62.0 0.7 %shard_map.114 = (bf16[192,256]{1,0:T(8,128)(2,1)}, bf16[192,256]{1,0:T(8,128)(2,1)}) custom-call(bf16[192,256]{1,0:T(8,128)(2,1)S(1)} %get-tuple-element.6.first, bf16[192,256]{1,0:T(8,128)(2,1)S(1)} %get-tuple-element.7.second), custom_call_target="tpu_custom_call" | custom-call | tf_op jit(solution)/shard_map/pallas_call | solution.py:527
